TPU v7x, 32 devices: a whole 2x2x4 slice. The times are simulated.
32 devices in a mesh: row: 8 (over y, x, core), col: 4 (over z).
Axes of the slice: x: 2, y: 2, z: 4, core: 2. Of those that a mesh axis runs over, the one named last changes fastest.
Arguments:
- built: bfloat16 [4096, 4096], P('row', 'col'), may hold values from -0.59765625 to 0.59765625
- build_order: int32 [32], replicated, may hold values from 0 to 31, each once
- p_pattern: int32 [32, 32], replicated, may hold values from 0 to 1, as said below
- q_pattern: int32 [32, 32], replicated, may hold values from 0 to 1, as said below
Outputs:
- purified: bfloat16 [4096, 4096], P('row', 'col')
Inputs may be any that keep to these rules, and one draw needn't show every extreme that they name: p_pattern is symmetric and 1 on the diagonal; p_pattern[i, j] is 0 unless the distance of i and j counted round the 32 blocks, or that of i and j + 16, is at most 1. q_pattern[i, j] is 0 unless the distance of i and j counted round the 32 blocks, or that of i and j + 16, is at most 2.
All inputs are finite; a program needn't handle non-finite values.
Results may differ from a plain program's by a relative error of at most 0.0045.
Values may be sent and summed in bfloat16 or wider, within the bound.
A program may use at most 128 MiB of HBM per device.

v0:
```python
import jax
import jax.numpy as jnp
from jax import lax
from jax.sharding import PartitionSpec as P

BS = 128


def contract(col_panel, portion):
    return jnp.dot(portion, col_panel, preferred_element_type=jnp.float32)


def body(built, build_order, p_pattern, q_pattern):
    row_count = built.shape[0] // BS
    col_count = built.shape[1] // BS
    block_count = build_order.shape[0]
    row_index = lax.axis_index("row")
    col_index = lax.axis_index("col")
    build_slab = lax.all_gather(built, "row", axis=0, tiled=True)
    blocks = build_slab.reshape(block_count, BS, col_count * BS)
    inverse = (
        jnp.zeros((block_count,), jnp.int32)
        .at[build_order]
        .set(jnp.arange(block_count, dtype=jnp.int32))
    )
    col_mask = lax.dynamic_slice_in_dim(p_pattern, col_index * col_count, col_count, 1).astype(
        jnp.bfloat16
    )
    ordered = blocks[inverse].reshape(block_count, BS, col_count, BS)
    columns = (ordered * col_mask[:, None, :, None]).reshape(block_count * BS, col_count * BS)
    start_block = row_index * row_count
    local_tile = lax.dynamic_slice_in_dim(columns, start_block * BS, row_count * BS, 0)
    q_block = lax.dynamic_slice(
        q_pattern, (start_block, col_index * col_count), (row_count, col_count)
    ).astype(jnp.float32)
    q_tile = jnp.broadcast_to(q_block[:, None, :, None], (row_count, BS, col_count, BS)).reshape(
        row_count * BS, col_count * BS
    )
    square = contract(columns, lax.all_gather(local_tile, "col", axis=1, tiled=True)) * q_tile
    rounded = square.astype(jnp.bfloat16)
    cubed_term = contract(columns, lax.all_gather(rounded, "col", axis=1, tiled=True))
    return ((3.0 * square - 2.0 * cubed_term) * q_tile).astype(jnp.bfloat16)


def solution(mesh):
    placed = (P("row", "col"), P(), P(), P())
    return jax.shard_map(
        body, mesh=mesh, in_specs=placed, out_specs=P("row", "col"), check_vma=False
    )
```

profile of v0, /device:TPU:0, one launch (start us, length us, event | category | flops | bytes accessed | tf_op | source)
XLA Modules:
  0.0 273.1 jit_solution(3212071331895305885)
XLA Ops:
  6.5 0.0 all-gather.4.cloned.1.call-start
  6.5 0.7 all-gather.4.cloned.1.call-update
  7.3 0.0 all-gather.6.cloned.1.call-start
  7.3 0.7 compare_select_fusion.1
  8.0 0.7 scatter_custom_fusion
  8.7 0.8 dynamic-slice_convert_fusion
  9.5 56.8 %all-gather.4.cloned.1.call-done = bf16[4096,1024]{1,0:T(8,128)(2,1)} async-done(((bf16[512,1024]{1,0:T(8,128)(2,1)}), bf16[4096,1024]{1,0:T(8,128)(2,1)}) %all-gather.4.cloned.1.call-update) | async-done | bytes 8388624 | tf_op jit(solution)/shard_map/all_gather | solution.py:19
  66.2 8.4 %gather_fusion = bf16[32,128,1024]{2,1,0:T(8,128)(2,1)} fusion(bf16[32,128,1024]{2,1,0:T(8,128)(2,1)} %bitcast.23, s32[1024]{0:T(1024)S(1)} %pad_clamp_fusion), kind=kCustom, calls=%fused_computation | custom fusion | bytes 16777344 | tf_op jit(solution)/shard_map/gather | solution.py:29
  74.6 0.0 copy-start
  74.7 1.1 mul.40
  75.8 2.2 copy-done
  78.0 1.9 bitcast_multiply_fusion
  79.9 0.0 copy-start.1
  80.0 3.2 %copy-done.1 = bf16[4096,1024]{1,0:T(8,128)(2,1)} copy-done((bf16[4096,1024]{1,0:T(8,128)(2,1)}, bf16[4096,1024]{1,0:T(8,128)(2,1)S(1)}, u32[]{:S(2)}) %copy-start.1) | copy-done | bytes 8388632
  83.2 1.0 constant_dynamic-slice_fusion
  84.2 0.0 all-gather.6.cloned.1.call-update
  84.2 0.0 all-gather.8.cloned.1.call-start
  84.3 0.8 dynamic-slice_convert_fusion.1
  85.1 80.1 %all-gather.6.cloned.1.call-done = bf16[512,4096]{1,0:T(8,128)(2,1)} async-done(((bf16[512,1024]{1,0:T(8,128)(2,1)}), bf16[512,4096]{1,0:T(8,128)(2,1)}) %all-gather.6.cloned.1.call-update) | async-done | bytes 4194320 | tf_op jit(solution)/shard_map/all_gather | solution.py:39
  165.1 0.2 broadcast_in_dim.15
  165.3 10.9 %fusion.1 = (bf16[512,1024]{1,0:T(8,128)(2,1)}, f32[512,1024]{1,0:T(8,128)}) fusion(f32[64,8,8,128]{3,2,1,0:T(8,128)S(1)} %bitcast.24, bf16[512,4096]{1,0:T(8,128)(2,1)} %all-gather.6.cloned.1.call-done, bf16[4096,1024]{1,0:T(8,128)(2,1)} %copy-done.1), kind=kOutput, calls=%fused_computation.6 | convolution fusion | flops 4296015872 | bytes 17825792 | tf_op jit(solution)/shard_map/dot_general | solution.py:10
  176.3 0.0 all-gather.8.cloned.1.call-update
  176.3 79.4 %all-gather.8.cloned.1.call-done = bf16[512,4096]{1,0:T(8,128)(2,1)} async-done(((bf16[512,1024]{1,0:T(8,128)(2,1)}), bf16[512,4096]{1,0:T(8,128)(2,1)}) %all-gather.8.cloned.1.call-update) | async-done | bytes 4194320 | tf_op jit(solution)/shard_map/all_gather | solution.py:41
  255.7 10.9 %fusion = bf16[512,1024]{1,0:T(8,128)(2,1)} fusion(f32[64,8,8,128]{3,2,1,0:T(8,128)S(1)} %bitcast.25, f32[512,1024]{1,0:T(8,128)} %get-tuple-element.6, bf16[512,4096]{1,0:T(8,128)(2,1)} %all-gather.8.cloned.1.call-done, bf16[4096,1024]{1,0:T(8,128)(2,1)} %copy-done.1), kind=kOutput, calls=%fused_computation.5 | convolution fusion | flops 4298113024 | bytes 17825792 | tf_op jit(solution)/shard_map/dot_general | solution.py:10
  (3 shorter events, 0.0 us)
Async XLA Ops:
  6.5 59.7 %all-gather.4.cloned.1.call-start = ((), (), s32[]{:S(2)}) async-start(), calls=%async_computation | async-start | bytes 9437184 | tf_op jit(solution)/shard_map/all_gather | solution.py:19
  7.3 157.9 %all-gather.6.cloned.1.call-start = ((), (), s32[]{:S(2)}) async-start(), calls=%async_computation.1 | async-start | bytes 5242880 | tf_op jit(solution)/shard_map/all_gather | solution.py:39
  74.6 3.4 %copy-start = (bf16[32,128,1024]{2,1,0:T(8,128)(2,1)S(1)}, bf16[32,128,1024]{2,1,0:T(8,128)(2,1)}, u32[]{:S(2)}) copy-start(bf16[32,128,1024]{2,1,0:T(8,128)(2,1)} %gather_fusion) | copy-start | bytes 25165828
  79.9 3.2 %copy-start.1 = (bf16[4096,1024]{1,0:T(8,128)(2,1)}, bf16[4096,1024]{1,0:T(8,128)(2,1)S(1)}, u32[]{:S(2)}) copy-start(bf16[4096,1024]{1,0:T(8,128)(2,1)S(1)} %bitcast_multiply_fusion) | copy-start | bytes 25165828
  84.2 171.4 %all-gather.8.cloned.1.call-start = ((), (), s32[]{:S(2)}) async-start(), calls=%async_computation.2 | async-start | bytes 5242880 | tf_op jit(solution)/shard_map/all_gather | solution.py:41
Sparse Core Ops, SparseCore 0:
  9.2 56.9 all-gather.3
  84.4 80.7 all-gather.5
  176.4 79.2 all-gather.7
where the time goes:
time: 273 us
  waiting for transfers between devices  217 us (79%)
  matrix products  21.8 us (8%)
  local copies, waits for them, and re-layouts  16.9 us (6%)
  between operations  13.2 us (5%)
  other arithmetic  4.14 us (2%)
    all_gather x1, waiting for transfers between devices, body(): lax.all_gather(local_tile, 'col', axis=1, tiled=True)  80.1 us
    all_gather x1, waiting for transfers between devices, body(): lax.all_gather(rounded, 'col', axis=1, tiled=True)  79.4 us
    all_gather x1, waiting for transfers between devices, body(): build_slab = lax.all_gather(built, 'row', axis=0, tiled=True)  56.8 us
    dot_general x2, matrix products, contract(): return jnp.dot(portion, col_panel, preferred_element_type=jnp.float32)  21.8 us
    gather x1, local copies, waits for them, and re-layouts, body(): ordered = blocks[inverse].reshape(block_count, BS, col_count, BS)  8.42 us
  transfers between devices with their start and end apart: 3, of which 3 were waited for; matrix products, arithmetic and copies ran while one was open for 1% of the time, Pallas kernels for 0%

commit v1 on v0

--- a/solution.py
+++ b/solution.py
@@ -1,9 +1,25 @@
+import functools
 import jax
 import jax.numpy as jnp
 from jax import lax
 from jax.sharding import PartitionSpec as P
 
 BS = 128
+
+
+def fit_pipes(vals, dev_axis):
+    g_now, long_array = (lax.axis_size(dev_axis), lax.axis_index(dev_axis))
+    state_now, res = (vals, 1)
+    while res < g_now:
+        even = lax.ppermute(state_now, dev_axis, tuple(((h, h ^ res) for h in range(g_now))))
+        near = jnp.concatenate([state_now, even], axis=1)
+        reply = jnp.concatenate([even, state_now], axis=1)
+        state_now = jnp.where(long_array & res == 0, near, reply)
+        res = 2 * res
+    return state_now
+
+
+_search_fields = functools.partial(fit_pipes, dev_axis="col")
 
 
 def contract(col_panel, portion):
@@ -36,7 +52,7 @@
     q_tile = jnp.broadcast_to(q_block[:, None, :, None], (row_count, BS, col_count, BS)).reshape(
         row_count * BS, col_count * BS
     )
-    square = contract(columns, lax.all_gather(local_tile, "col", axis=1, tiled=True)) * q_tile
+    square = contract(columns, _search_fields(local_tile)) * q_tile
     rounded = square.astype(jnp.bfloat16)
     cubed_term = contract(columns, lax.all_gather(rounded, "col", axis=1, tiled=True))
     return ((3.0 * square - 2.0 * cubed_term) * q_tile).astype(jnp.bfloat16)

time: 273 us -> 315 us (1.15)
  waiting for transfers between devices: 217 us -> 252 us
  starting transfers between devices: 0.08 us -> 4.06 us
    ppermute x0 -> x2, waiting for transfers between devices: none -> 114 us  [fit_pipes(): lax.ppermute(state_now, dev_axis, tuple(((h, h ^ res) for h in range(g_no...]
    all_gather x1 -> x0, waiting for transfers between devices: 80.1 us -> none  [body(): lax.all_gather(local_tile, 'col', axis=1, tiled=True)]
    ppermute x0 -> x2, starting transfers between devices: none -> 4.02 us  [fit_pipes(): lax.ppermute(state_now, dev_axis, tuple(((h, h ^ res) for h in range(g_no...]
  transfers between devices with their start and end apart: 3 -> 4, of which waited for: 3 -> 4; matrix products, arithmetic and copies ran while one was open for 1% -> 1% of each run, Pallas kernels for 0% -> 0%
where the time goes in v1:
time: 315 us
  waiting for transfers between devices  252 us (80%)
  matrix products  23 us (7%)
  local copies, waits for them, and re-layouts  16 us (5%)
  between operations  13.5 us (4%)
  other arithmetic  6.53 us (2%)
  starting transfers between devices  4.06 us (1%)
    ppermute x2, waiting for transfers between devices, fit_pipes(): lax.ppermute(state_now, dev_axis, tuple(((h, h ^ res) for h in range(g_no...  114 us
    all_gather x1, waiting for transfers between devices, body(): lax.all_gather(rounded, 'col', axis=1, tiled=True)  80.9 us
    all_gather x1, waiting for transfers between devices, body(): build_slab = lax.all_gather(built, 'row', axis=0, tiled=True)  56.8 us
    dot_general x2, matrix products, contract(): return jnp.dot(portion, col_panel, preferred_element_type=jnp.float32)  23 us
    gather x1, local copies, waits for them, and re-layouts, body(): ordered = blocks[inverse].reshape(block_count, BS, col_count, BS)  8.42 us
  transfers between devices with their start and end apart: 4, of which 4 were waited for; matrix products, arithmetic and copies ran while one was open for 1% of the time, Pallas kernels for 0%

profile of v1, /device:TPU:0, one launch (start us, length us, event | category | flops | bytes accessed | tf_op | source)
XLA Modules:
  0.0 315.1 jit_solution(16737250623659351148)
XLA Ops:
  6.5 0.0 all-gather.3.cloned.1.call-start
  6.5 0.7 all-gather.3.cloned.1.call-update
  7.3 0.0 all-gather.5.cloned.1.call-start
  7.3 0.7 compare_select_fusion.1
  8.0 0.7 scatter_custom_fusion
  8.7 0.8 dynamic-slice_convert_fusion
  9.5 56.8 %all-gather.3.cloned.1.call-done = bf16[4096,1024]{1,0:T(8,128)(2,1)} async-done(((bf16[512,1024]{1,0:T(8,128)(2,1)}), bf16[4096,1024]{1,0:T(8,128)(2,1)}) %all-gather.3.cloned.1.call-update) | async-done | bytes 8388624 | tf_op jit(solution)/shard_map/all_gather | solution.py:35
  66.2 8.4 %gather_fusion = bf16[32,128,1024]{2,1,0:T(8,128)(2,1)} fusion(bf16[32,128,1024]{2,1,0:T(8,128)(2,1)} %bitcast.22, s32[1024]{0:T(1024)S(1)} %pad_clamp_fusion), kind=kCustom, calls=%fused_computation | custom fusion | bytes 16777344 | tf_op jit(solution)/shard_map/gather | solution.py:45
  74.6 0.0 copy-start
  74.7 1.1 mul.40
  75.8 2.2 copy-done
  78.0 1.9 bitcast_multiply_fusion
  79.9 0.0 copy-start.1
  80.0 3.2 %copy-done.1 = bf16[4096,1024]{1,0:T(8,128)(2,1)} copy-done((bf16[4096,1024]{1,0:T(8,128)(2,1)}, bf16[4096,1024]{1,0:T(8,128)(2,1)S(1)}, u32[]{:S(2)}) %copy-start.1) | copy-done | bytes 8388632
  83.2 0.1 constant_dynamic-slice_fusion
  83.2 1.6 collective-permute-start
  84.8 23.9 %collective-permute-done = bf16[512,1024]{1,0:T(8,128)(2,1)} collective-permute-done((bf16[512,1024]{1,0:T(8,128)(2,1)S(1)}, bf16[512,1024]{1,0:T(8,128)(2,1)}, u32[]{:S(2)}, u32[]{:S(2)}) %collective-permute-start) | collective-permute-done | bytes 1048608 | tf_op jit(solution)/shard_map/ppermute | solution.py:14
  108.7 2.4 maximum_select_fusion.2
  111.1 0.0 copy-start.2
  111.1 2.5 collective-permute-start.1
  113.6 0.8 dynamic-slice_convert_fusion.1
  114.4 0.0 copy-done.2
  114.4 89.7 %collective-permute-done.1 = bf16[512,2048]{1,0:T(8,128)(2,1)} collective-permute-done((bf16[512,2048]{1,0:T(8,128)(2,1)S(1)}, bf16[512,2048]{1,0:T(8,128)(2,1)}, u32[]{:S(2)}, u32[]{:S(2)}) %collective-permute-start.1) | collective-permute-done | bytes 2097184 | tf_op jit(solution)/shard_map/ppermute | solution.py:14
  204.1 0.2 broadcast_in_dim.15
  204.3 12.1 %fusion.8 = (bf16[512,1024]{1,0:T(8,128)(2,1)}, f32[512,1024]{1,0:T(8,128)}) fusion(f32[64,8,8,128]{3,2,1,0:T(8,128)S(1)} %bitcast.23, bf16[4096,1024]{1,0:T(8,128)(2,1)} %copy-done.1, bf16[512,2048]{1,0:T(8,128)(2,1)} %collective-permute-done.1, bf16[512,2048]{1,0:T(8,128)(2,1)} %copy-done.2, pred[]{:T(512)S(6)} %eq.6), kind=kOutput, calls=%fused_computation.15 | convolution fusion | flops 4314890240 | bytes 17825792 | tf_op jit(solution)/shard_map/dot_general | solution.py:26
  216.4 0.0 all-gather.5.cloned.1.call-update
  216.4 80.9 %all-gather.5.cloned.1.call-done = bf16[512,4096]{1,0:T(8,128)(2,1)} async-done(((bf16[512,1024]{1,0:T(8,128)(2,1)}), bf16[512,4096]{1,0:T(8,128)(2,1)}) %all-gather.5.cloned.1.call-update) | async-done | bytes 4194320 | tf_op jit(solution)/shard_map/all_gather | solution.py:57
  297.3 10.9 %fusion.7 = bf16[512,1024]{1,0:T(8,128)(2,1)} fusion(f32[64,8,8,128]{3,2,1,0:T(8,128)S(1)} %bitcast.24, f32[512,1024]{1,0:T(8,128)} %get-tuple-element.6, bf16[512,4096]{1,0:T(8,128)(2,1)} %all-gather.5.cloned.1.call-done, bf16[4096,1024]{1,0:T(8,128)(2,1)} %copy-done.1), kind=kOutput, calls=%fused_computation.13 | convolution fusion | flops 4298113024 | bytes 17825792 | tf_op jit(solution)/shard_map/dot_general | solution.py:26
  (3 shorter events, 0.0 us)
Async XLA Ops:
  6.5 59.7 %all-gather.3.cloned.1.call-start = ((), (), s32[]{:S(2)}) async-start(), calls=%async_computation | async-start | bytes 9437184 | tf_op jit(solution)/shard_map/all_gather | solution.py:35
  7.3 290.1 %all-gather.5.cloned.1.call-start = ((), (), s32[]{:S(2)}) async-start(), calls=%async_computation.1 | async-start | bytes 5242880 | tf_op jit(solution)/shard_map/all_gather | solution.py:57
  74.6 3.4 %copy-start = (bf16[32,128,1024]{2,1,0:T(8,128)(2,1)S(1)}, bf16[32,128,1024]{2,1,0:T(8,128)(2,1)}, u32[]{:S(2)}) copy-start(bf16[32,128,1024]{2,1,0:T(8,128)(2,1)} %gather_fusion) | copy-start | bytes 25165828
  79.9 3.2 %copy-start.1 = (bf16[4096,1024]{1,0:T(8,128)(2,1)}, bf16[4096,1024]{1,0:T(8,128)(2,1)S(1)}, u32[]{:S(2)}) copy-start(bf16[4096,1024]{1,0:T(8,128)(2,1)S(1)} %bitcast_multiply_fusion) | copy-start | bytes 25165828
  83.2 25.5 %collective-permute-start = (bf16[512,1024]{1,0:T(8,128)(2,1)S(1)}, bf16[512,1024]{1,0:T(8,128)(2,1)}, u32[]{:S(2)}, u32[]{:S(2)}) collective-permute-start(bf16[512,1024]{1,0:T(8,128)(2,1)S(1)} %constant_dynamic-slice_fusion), channel_id=1, source_target_pairs={{0,1},{1,0},{2,3},{3,2},{4,5},{5,4},{6,7},{7,6},{8,9},{9,8},{10,11... | collective-permute-start | bytes 3145736 | tf_op jit(solution)/shard_map/ppermute | solution.py:14
  111.1 3.2 %copy-start.2 = (bf16[512,2048]{1,0:T(8,128)(2,1)}, bf16[512,2048]{1,0:T(8,128)(2,1)S(1)}, u32[]{:S(2)}) copy-start(bf16[512,2048]{1,0:T(8,128)(2,1)S(1)} %maximum_select_fusion.2) | copy-start | bytes 6291460
  111.1 92.9 %collective-permute-start.1 = (bf16[512,2048]{1,0:T(8,128)(2,1)S(1)}, bf16[512,2048]{1,0:T(8,128)(2,1)}, u32[]{:S(2)}, u32[]{:S(2)}) collective-permute-start(bf16[512,2048]{1,0:T(8,128)(2,1)S(1)} %maximum_select_fusion.2), channel_id=1, source_target_pairs={{0,2},{1,3},{2,0},{3,1},{4,6},{5,7},{6,4},{7,5},{8,10},{9,11},{10,... | collective-permute-start | bytes 6291464 | tf_op jit(solution)/shard_map/ppermute | solution.py:14
Sparse Core Ops, SparseCore 0:
  9.2 56.9 all-gather.2
  216.6 80.7 all-gather.4
